TPU v7x, 768 devices: a whole 4x8x12 slice. The times are simulated.
768 devices in a mesh: st: 24 (over x, z_hi, core), fifth: 32 (over y, z_lo).
Axes of the slice: x: 4, y: 8, z: 12 (z_hi: 3, z_lo: 4; z = z_hi * 4 + z_lo), core: 2. Of those that a mesh axis runs over, the one named last changes fastest.
Arguments:
- source_field: float32 [2, 4, 3, 32, 24, 4096], P(None, None, None, 'fifth', 'st'), may hold values from -6 to 6
- gauge_rows: float32 [2, 4, 2, 3, 24, 4096], P(None, None, None, None, 'st', 'fifth'), may hold values from -3 to 3
Outputs:
- applied_once: float32 [2, 4, 3, 32, 24, 4096], P(None, None, None, 'fifth', 'st')
- applied_twice: float32 [2, 4, 3, 32, 24, 4096], P(None, None, None, 'fifth', 'st')
All inputs are finite; a program needn't handle non-finite values.
Results may differ from a plain program's by a relative error of at most 0.00002.
Values sent between devices are 32-bit elements; how exact they have to be, the bound alone decides.
No kernel may reach another device: no remote copies, remote signals or barrier semaphores. Data moves between devices by JAX's collectives and lax.ppermute only.
A program may use at most 32 MiB of HBM per device.

v0:
```python
import functools

import jax
import jax.numpy as jnp
from jax import lax
from jax.experimental import pallas as pl
from jax.experimental.pallas import tpu as pltpu
from jax.sharding import PartitionSpec as P


WALL_HEIGHT = 1.8
QUARK_MASS = 0.5
KS = range(4)
RUN = 4
F32 = jnp.float32


def cmul(a, b):
    return a[0] * b[0] - a[1] * b[1], a[0] * b[1] + a[1] * b[0]


def cmul_conj(a, b):
    return a[0] * b[0] + a[1] * b[1], a[0] * b[1] - a[1] * b[0]


def cadd(a, b):
    return a[0] + b[0], a[1] + b[1]


def csub(a, b):
    return a[0] - b[0], a[1] - b[1]


def times_i(a):
    return -a[1], a[0]


def neg(a):
    return -a[0], -a[1]


def row_source(direction, spin):
    if direction == 0:
        return 1 - spin, times_i
    if direction == 1:
        return (1, lambda a: a) if spin == 0 else (0, neg)
    return (0, times_i) if spin == 0 else (1, lambda a: neg(times_i(a)))


def link_index(part, mu, row, col):
    return ((part * 4 + mu) * 2 + row) * 3 + col


TIME_BLOCK = ((18, 24), (42, 48))
SPACE_BLOCK = ((0, 18), (24, 42))
PLACES = {}
for number, spans in enumerate((TIME_BLOCK, SPACE_BLOCK)):
    filled = 0
    for low, high in spans:
        for component in range(low, high):
            PLACES[component] = (number, filled)
            filled += 1


def block_rows(spans):
    return sum(high - low for low, high in spans)


def third_row(rows):
    out = []
    for a in range(3):
        b, c = (a + 1) % 3, (a + 2) % 3
        re, im = csub(cmul(rows[0][b], rows[1][c]), cmul(rows[0][c], rows[1][b]))
        out.append((re, -im))
    return out


def complete(blocks, directions, links):
    for n, mu in enumerate(directions):
        for k in KS:

            def entry(p, r, c):
                number, place = PLACES[link_index(p, mu, r, c)]
                block = blocks[number]
                rows = block.shape[0] // 32
                return block[pl.ds(k * rows + place, 8, stride=4 * rows), :]

            rows = [[(entry(0, r, c), entry(1, r, c)) for c in range(3)] for r in range(2)]
            rows.append(third_row(rows))
            for r in range(3):
                for c in range(3):
                    for p in range(2):
                        links[n, (r * 3 + c) * 2 + p, k] = rows[r][c][p]


def load_link(links, mu, k):
    ref, n = (links[0], mu) if mu < 3 else (links[1], 0)
    return [
        [(ref[n, (r * 3 + c) * 2, k], ref[n, (r * 3 + c) * 2 + 1, k]) for c in range(3)]
        for r in range(3)
    ]


def apply_link(link, half):
    out = []
    for a in range(3):
        total = cmul(link[a][0], half[0])
        for b in (1, 2):
            total = cadd(total, cmul(link[a][b], half[b]))
        out.append(total)
    return out


def apply_adjoint(link, half):
    out = []
    for a in range(3):
        total = cmul_conj(link[0][a], half[0])
        for b in (1, 2):
            total = cadd(total, cmul_conj(link[b][a], half[b]))
        out.append(total)
    return out


def comp(part, spin, colour):
    return (part * 4 + spin) * 3 + colour


def hcomp(part, spin, colour):
    return (part * 2 + spin) * 3 + colour


def get(ref, k, spin):
    at = pl.ds(k, 8, stride=4)
    return [(ref[comp(0, spin, c), at, :], ref[comp(1, spin, c), at, :]) for c in range(3)]


def get_half(ref, k, spin):
    at = pl.ds(8 * k, 8)
    return [(ref[hcomp(0, spin, c), at, :], ref[hcomp(1, spin, c), at, :]) for c in range(3)]


def put_half(ref, k, spin, values):
    at = pl.ds(8 * k, 8)
    for c in range(3):
        ref[hcomp(0, spin, c), at, :] = values[c][0]
        ref[hcomp(1, spin, c), at, :] = values[c][1]


def project(v, k, mu, spin, sign):
    source, factor = row_source(mu, spin)
    upper = get(v, k, spin)
    lower = get(v, k, 2 + source)
    op = cadd if sign > 0 else csub
    return [op(upper[c], factor(lower[c])) for c in range(3)]


def both(fn, *values):
    return [tuple(fn(*(v[c][p] for v in values)) for p in range(2)) for c in range(3)]


def shift_ahead(mu, k, here, other, lane):
    if mu == 0:
        return both(
            lambda h: jnp.where(lane % 16 < 15, pltpu.roll(h, 127, 1), pltpu.roll(h, 15, 1)), here
        )
    if mu == 1:
        return both(lambda h, o: pltpu.roll(jnp.where(lane >= 16, h, o), 112, 1), here, other)
    return other if k < 2 else both(lambda o: pltpu.roll(o, 7, 0), other)


def shift_behind(mu, k, here, other, lane):
    if mu == 0:
        return both(
            lambda h: jnp.where(lane % 16 > 0, pltpu.roll(h, 1, 1), pltpu.roll(h, 113, 1)), here
        )
    if mu == 1:
        return both(lambda h, o: pltpu.roll(jnp.where(lane < 112, h, o), 16, 1), here, other)
    return other if k >= 2 else both(lambda o: pltpu.roll(o, 1, 0), other)


def pick(test, a, b):
    return both(lambda x, y: jnp.where(test, x, y), a, b)


def put_swapped(first, second, k, spin, even, up, down):
    put_half(first, k, spin, pick(even, up, down))
    put_half(second, k, spin, pick(even, down, up))


def even_at(axis):
    return lax.rem(lax.axis_index(axis), 2) == 0


def factors():
    t, s = lax.axis_index("st"), lax.axis_index("fifth")
    nt, ns = lax.axis_size("st"), lax.axis_size("fifth")
    pick = lambda test, value: jnp.where(test, jnp.float32(value), jnp.float32(1.0))
    return (
        pick(t == nt - 1, -1.0),
        pick(t == 0, -1.0),
        pick(s == ns - 1, -QUARK_MASS),
        pick(s == 0, -QUARK_MASS),
    )


def spatial(v, links, moved):
    lane = lax.broadcasted_iota(jnp.int32, (8, 128), 1)
    for k in KS:
        for mu in (1, 2):
            link = load_link(links, mu, k)
            for spin in range(2):
                w = apply_adjoint(link, project(v, k, mu, spin, -1))
                put_half(moved.at[mu - 1], k, spin, w)
    for k in KS:
        hops = [None] * 4
        for mu in range(3):
            link = load_link(links, mu, k)
            partner = (k, k ^ 1, k ^ 2)[mu]
            for spin in range(2):
                here = project(v, k, mu, spin, 1) if mu < 2 else None
                other = project(v, partner, mu, spin, 1) if mu > 0 else None
                fwd = apply_link(link, shift_ahead(mu, k, here, other, lane))
                if mu == 0:
                    w, w_other = apply_adjoint(link, project(v, k, 0, spin, -1)), None
                else:
                    w = get_half(moved.at[mu - 1], k, spin) if mu == 1 else None
                    w_other = get_half(moved.at[mu - 1], partner, spin)
                add_hop(hops, spin, fwd, shift_behind(mu, k, w, w_other, lane), mu)
        yield k, hops


def add_hop(hops, spin, fwd, bwd, mu):
    def add(at, value):
        hops[at] = value if hops[at] is None else both(lambda a, b: a + b, hops[at], value)

    add(spin, both(lambda a, b: a + b, fwd, bwd))
    diff = both(lambda a, b: b - a, fwd, bwd)
    if mu == 3:
        add(2 + spin, diff)
    else:
        target = next(s for s in range(2) if row_source(mu, s)[0] == spin)
        add(2 + target, [row_source(mu, target)[1](d) for d in diff])


def put_field(out, k, values):
    at = pl.ds(k, 8, stride=4)
    for spin in range(4):
        for c in range(3):
            for p in range(2):
                out[comp(p, spin, c), at, :] = values[spin][c][p]


def finish(v, k, hops, links, time1, time2, fifth1, fifth2):
    even_t, even_s = even_at("st"), even_at("fifth")
    time_last, time_first, fifth_last, fifth_first = factors()
    link = load_link(links, 3, k)
    for spin in range(2):
        got1, got2 = get_half(time1, k, spin), get_half(time2, k, spin)
        fwd = apply_link(link, both(lambda a: a * time_last, pick(even_t, got1, got2)))
        bwd = both(lambda a: a * time_first, pick(even_t, got2, got1))
        add_hop(hops, spin, fwd, bwd, 3)
    result = []
    for spin in range(4):
        got1, got2 = get_half(fifth1, k, spin % 2), get_half(fifth2, k, spin % 2)
        if spin < 2:
            chiral, factor = pick(even_s, got2, got1), fifth_first
        else:
            chiral, factor = pick(even_s, got1, got2), fifth_last
        result.append(
            both(
                lambda a, h, c: (5.0 - WALL_HEIGHT) * a - 0.5 * h - c * factor,
                get(v, k, spin), hops[spin], chiral,
            )
        )
    return result


def put_time(time1, time2, k, spin, upper, lower, link):
    diff = both(lambda a, b: a - b, upper, lower)
    moved = apply_adjoint(link, both(lambda a, b: a + b, upper, lower))
    put_swapped(time1, time2, k, spin, even_at("st"), moved, diff)


def fifth_sends(v, fifth1, fifth2):
    for k in KS:
        for spin in range(2):
            put_swapped(fifth1, fifth2, k, spin, even_at("fifth"), get(v, k, spin), get(v, k, 2 + spin))


def time_sends(v, time_block, time1, time2, links):
    complete((time_block, None), (3,), links)
    for k in KS:
        link = load_link((None, links), 3, k)
        for spin in range(2):
            put_time(time1, time2, k, spin, get(v, k, spin), get(v, k, 2 + spin), link)


def first_local(v, time_block, space_block, space_links, hops_out, moved):
    complete((time_block, space_block), range(3), space_links)
    for k, hops in spatial(v, (space_links, None), moved):
        put_field(hops_out, k, hops)


def first_kernel(
    v, hops_in, time_links, time1, time2, fifth1, fifth2,
    kept, time1_out, time2_out, fifth1_out, fifth2_out,
):
    links = (None, time_links)
    for k in KS:
        hops = [get(hops_in, k, spin) for spin in range(4)]
        result = finish(v, k, hops, links, time1, time2, fifth1, fifth2)
        put_field(kept, k, result)
        link = load_link(links, 3, k)
        for spin in range(2):
            upper, lower = result[spin], result[2 + spin]
            put_time(time1_out, time2_out, k, spin, upper, lower, link)
            put_swapped(fifth1_out, fifth2_out, k, spin, even_at("fifth"), upper, lower)


def second_local(v, space_links, out, hops_out, moved):
    out[...] = v[...]
    for k, hops in spatial(v, (space_links, None), moved):
        put_field(hops_out, k, hops)


def second_kernel(v, hops_in, time_links, time1, time2, fifth1, fifth2, out):
    for k in KS:
        hops = [get(hops_in, k, spin) for spin in range(4)]
        put_field(out, k, finish(v, k, hops, (None, time_links), time1, time2, fifth1, fifth2))


def ring_copies(spans, run_rows, out):
    filled = 0
    for place in range(RUN):
        for low, high in spans:
            out[0, pl.ds(filled, high - low), :] = run_rows[place, pl.ds(low, high - low), :]
            filled += high - low
    for i in range(1, out.shape[0]):
        out[i] = out[0]


FIELD = jax.ShapeDtypeStruct((24, 32, 128), F32)
HALF = jax.ShapeDtypeStruct((12, 32, 128), F32)
SPACE_LINKS = jax.ShapeDtypeStruct((3, 18, 4, 8, 128), F32)
TIME_LINKS = jax.ShapeDtypeStruct((1, 18, 4, 8, 128), F32)
MOVED = pltpu.VMEM((2, 12, 32, 128), F32)


def run(kernel, outs, scratch, *args):
    size = 4 * sum(a.size for a in args) + 4 * sum(o.size for o in outs)
    vmem = pl.BlockSpec(memory_space=pltpu.VMEM)
    return pl.pallas_call(
        kernel,
        out_shape=outs,
        in_specs=[vmem] * len(args),
        out_specs=[vmem] * len(outs),
        scratch_shapes=scratch,
        cost_estimate=pl.CostEstimate(flops=20_000_000, bytes_accessed=size, transcendentals=0),
        compiler_params=pltpu.CompilerParams(vmem_limit_bytes=24 << 20),
    )(*args)


def trade(block, axis, round):
    count = lax.axis_size(axis)
    step = 1 if round == 1 else -1
    route = [(i, (i + (step if i % 2 == 0 else -step)) % count) for i in range(count)]
    return lax.ppermute(block, axis, route)


def traded(copies, groups):
    return lax.all_to_all(copies, "fifth", 0, 0, axis_index_groups=groups, tiled=False)


def ring_traded(copies, groups):
    got = traded(copies, groups)
    return got.reshape(got.shape[0] * got.shape[1], 128)


def on_device(source_field, gauge_rows):
    v = source_field.reshape(24, 32, 128)
    count = lax.axis_size("fifth")
    runs = [list(range(i, i + RUN)) for i in range(0, count, RUN)]
    rings = [list(range(i, count, RUN)) for i in range(RUN)]
    own = jnp.broadcast_to(gauge_rows.reshape(1, 48, 128), (RUN, 48, 128))
    run_rows = traded(own, runs)
    time_copies, space_copies = (
        run(
            functools.partial(ring_copies, spans),
            (jax.ShapeDtypeStruct((count // RUN, RUN * block_rows(spans), 128), F32),), [], run_rows,
        )[0]
        for spans in (TIME_BLOCK, SPACE_BLOCK)
    )
    time_block = ring_traded(time_copies, rings)
    fifth1, fifth2 = run(fifth_sends, (HALF,) * 2, [], v)
    fifth1 = trade(fifth1, "fifth", 1)
    fifth2 = trade(fifth2, "fifth", 2)
    space_block = ring_traded(space_copies, rings)
    time1, time2, time_links = run(time_sends, (HALF, HALF, TIME_LINKS), [], v, time_block)
    time1 = trade(time1, "st", 1)
    time2 = trade(time2, "st", 2)
    space_links, hops = run(first_local, (SPACE_LINKS, FIELD), [MOVED], v, time_block, space_block)
    kept, time1, time2, fifth1, fifth2 = run(
        first_kernel, (FIELD, HALF, HALF, HALF, HALF), [], v, hops, time_links, time1, time2, fifth1, fifth2
    )
    time1 = trade(time1, "st", 1)
    time2 = trade(time2, "st", 2)
    fifth1 = trade(fifth1, "fifth", 1)
    fifth2 = trade(fifth2, "fifth", 2)
    once, hops = run(second_local, (FIELD, FIELD), [MOVED], kept, space_links)
    (twice,) = run(second_kernel, (FIELD,), [], kept, hops, time_links, time1, time2, fifth1, fifth2)
    shape = source_field.shape
    return once.reshape(shape), twice.reshape(shape)


def solution(mesh):
    in_specs = (P(None, None, None, "fifth", "st", None), P(None, None, None, None, "st", "fifth"))
    out_specs = (P(None, None, None, "fifth", "st", None), P(None, None, None, "fifth", "st", None))

    return jax.shard_map(on_device, mesh=mesh, in_specs=in_specs, out_specs=out_specs, check_vma=False)
```

profile of v0, /device:TPU:1, one launch (start us, length us, event | category | flops | bytes accessed | tf_op | source)
XLA Modules:
  0.0 94.6 jit_solution(11052637526456236289)
XLA Ops:
  0.6 0.7 broadcast_in_dim.8
  1.4 12.3 %all_to_all.15.run_rows = f32[4,48,128]{2,1,0:T(8,128)S(1)} all-to-all(f32[4,48,128]{2,1,0:T(8,128)S(1)} %broadcast_in_dim.8), channel_id=1, replica_groups={{0,1,2,3},{4,5,6,7},{8,9,10,11},{12,13,14,15},{16,17,18,19},{20,21,22,2..., dimensions={0} | all-to-all | bytes 196608 | tf_op jit(solution)/shard_map/all_to_all | solution.py:371
  13.6 0.7 shard_map.41
  14.3 6.8 %all-to-all-start.1 = ((f32[8,48,128]{2,1,0:T(8,128)}), f32[8,48,128]{2,1,0:T(8,128)S(1)}, u32[]{:S(2)}, u32[]{:S(2)}) async-start(f32[8,48,128]{2,1,0:T(8,128)} %shard_map.41), calls=%async_computation.1 | async-start | bytes 393216 | tf_op jit(solution)/shard_map/all_to_all | solution.py:371
  21.2 0.9 shard_map.42
  22.0 0.0 copy-start
  22.0 7.9 %all-to-all-done.1 = f32[8,48,128]{2,1,0:T(8,128)S(1)} async-done(((f32[8,48,128]{2,1,0:T(8,128)}), f32[8,48,128]{2,1,0:T(8,128)S(1)}, u32[]{:S(2)}, u32[]{:S(2)}) %all-to-all-start.1) | async-done | bytes 196640 | tf_op jit(solution)/shard_map/all_to_all | solution.py:371
  29.9 3.5 %all-to-all-start.2 = ((f32[8,144,128]{2,1,0:T(8,128)}), f32[8,144,128]{2,1,0:T(8,128)S(1)}, u32[]{:S(2)}, u32[]{:S(2)}) async-start(f32[8,144,128]{2,1,0:T(8,128)} %shard_map.42), calls=%async_computation.2 | async-start | bytes 1179648 | tf_op jit(solution)/shard_map/all_to_all | solution.py:371
  33.4 0.0 copy-done
  33.4 0.1 shard_map.45
  33.5 2.8 %collective-permute-start.2 = (f32[12,32,128]{2,1,0:T(8,128)S(1)}, f32[12,32,128]{2,1,0:T(8,128)S(1)}, u32[]{:S(2)}, u32[]{:S(2)}) collective-permute-start(f32[12,32,128]{2,1,0:T(8,128)S(1)} %get-tuple-element.20), channel_id=1, source_target_pairs={{0,1},{1,0},{2,3},{3,2},{4,5},{5,4},{6,7},{7,6},{8,9},{9,8},{10,11... | collective-permute-start | bytes 589832 | tf_op jit(solution)/shard_map/ppermute | solution.py:367
  36.3 5.3 %collective-permute-start.3 = (f32[12,32,128]{2,1,0:T(8,128)S(1)}, f32[12,32,128]{2,1,0:T(8,128)S(1)}, u32[]{:S(2)}, u32[]{:S(2)}) collective-permute-start(f32[12,32,128]{2,1,0:T(8,128)S(1)} %get-tuple-element.21), channel_id=1, source_target_pairs={{0,31},{1,2},{2,1},{3,4},{4,3},{5,6},{6,5},{7,8},{8,7},{9,10},{10,... | collective-permute-start | bytes 589832 | tf_op jit(solution)/shard_map/ppermute | solution.py:367
  41.7 0.2 shard_map.44
  41.9 6.4 %collective-permute-start = (f32[12,32,128]{2,1,0:T(8,128)S(1)}, f32[12,32,128]{2,1,0:T(8,128)S(1)}, u32[]{:S(2)}, u32[]{:S(2)}) collective-permute-start(f32[12,32,128]{2,1,0:T(8,128)S(1)} %get-tuple-element.18), channel_id=1, source_target_pairs={{0,32},{32,0},{64,96},{96,64},{128,160},{160,128},{192,224},{224,1... | collective-permute-start | bytes 589832 | tf_op jit(solution)/shard_map/ppermute | solution.py:367
  48.3 9.7 %collective-permute-start.1 = (f32[12,32,128]{2,1,0:T(8,128)S(1)}, f32[12,32,128]{2,1,0:T(8,128)S(1)}, u32[]{:S(2)}, u32[]{:S(2)}) collective-permute-start(f32[12,32,128]{2,1,0:T(8,128)S(1)} %get-tuple-element.19), channel_id=1, source_target_pairs={{0,736},{32,64},{64,32},{96,128},{128,96},{160,192},{192,160},{224... | collective-permute-start | bytes 589832 | tf_op jit(solution)/shard_map/ppermute | solution.py:367
  58.0 0.0 all-to-all-done.2
  58.0 0.9 shard_map.43
  58.9 0.0 collective-permute-done.2.fifth1
  58.9 0.0 collective-permute-done.3.fifth2
  58.9 0.0 collective-permute-done.time1
  58.9 7.9 %collective-permute-done.1.time2 = f32[12,32,128]{2,1,0:T(8,128)S(1)} collective-permute-done((f32[12,32,128]{2,1,0:T(8,128)S(1)}, f32[12,32,128]{2,1,0:T(8,128)S(1)}, u32[]{:S(2)}, u32[]{:S(2)}) %collective-permute-start.1) | collective-permute-done | bytes 196640 | tf_op jit(solution)/shard_map/ppermute | solution.py:367
  66.8 0.4 shard_map.46
  67.2 6.7 %collective-permute-start.4 = (f32[12,32,128]{2,1,0:T(8,128)S(1)}, f32[12,32,128]{2,1,0:T(8,128)S(1)}, u32[]{:S(2)}, u32[]{:S(2)}) collective-permute-start(f32[12,32,128]{2,1,0:T(8,128)S(1)} %get-tuple-element.26), channel_id=1, source_target_pairs={{0,32},{32,0},{64,96},{96,64},{128,160},{160,128},{192,224},{224,1... | collective-permute-start | bytes 589832 | tf_op jit(solution)/shard_map/ppermute | solution.py:367
  73.9 2.5 %collective-permute-start.5 = (f32[12,32,128]{2,1,0:T(8,128)S(1)}, f32[12,32,128]{2,1,0:T(8,128)S(1)}, u32[]{:S(2)}, u32[]{:S(2)}) collective-permute-start(f32[12,32,128]{2,1,0:T(8,128)S(1)} %get-tuple-element.27), channel_id=1, source_target_pairs={{0,736},{32,64},{64,32},{96,128},{128,96},{160,192},{192,160},{224... | collective-permute-start | bytes 589832 | tf_op jit(solution)/shard_map/ppermute | solution.py:367
  76.4 1.9 %collective-permute-start.6 = (f32[12,32,128]{2,1,0:T(8,128)S(1)}, f32[12,32,128]{2,1,0:T(8,128)S(1)}, u32[]{:S(2)}, u32[]{:S(2)}) collective-permute-start(f32[12,32,128]{2,1,0:T(8,128)S(1)} %get-tuple-element.28), channel_id=1, source_target_pairs={{0,1},{1,0},{2,3},{3,2},{4,5},{5,4},{6,7},{7,6},{8,9},{9,8},{10,11... | collective-permute-start | bytes 589832 | tf_op jit(solution)/shard_map/ppermute | solution.py:367
  78.3 4.5 %collective-permute-start.7 = (f32[12,32,128]{2,1,0:T(8,128)S(1)}, f32[12,32,128]{2,1,0:T(8,128)S(1)}, u32[]{:S(2)}, u32[]{:S(2)}) collective-permute-start(f32[12,32,128]{2,1,0:T(8,128)S(1)} %get-tuple-element.29), channel_id=1, source_target_pairs={{0,31},{1,2},{2,1},{3,4},{4,3},{5,6},{6,5},{7,8},{8,7},{9,10},{10,... | collective-permute-start | bytes 589832 | tf_op jit(solution)/shard_map/ppermute | solution.py:367
  82.8 1.4 %shard_map.47 = (f32[24,32,128]{2,1,0:T(8,128)}, f32[24,32,128]{2,1,0:T(8,128)S(1)}) custom-call(f32[24,32,128]{2,1,0:T(8,128)S(1)} %get-tuple-element.22.v, f32[3,18,4,8,128]{4,3,2,1,0:T(8,128)S(1)} %get-tuple-element.23.space_links), custom_call_target="tpu_custom_call" | custom-call | flops 20000000 | bytes 2064384 | tf_op jit(solution)/shard_map/pallas_call | solution.py:352
  84.2 0.0 collective-permute-done.4.time1
  84.2 1.7 %collective-permute-done.5.time2 = f32[12,32,128]{2,1,0:T(8,128)S(1)} collective-permute-done((f32[12,32,128]{2,1,0:T(8,128)S(1)}, f32[12,32,128]{2,1,0:T(8,128)S(1)}, u32[]{:S(2)}, u32[]{:S(2)}) %collective-permute-start.5) | collective-permute-done | bytes 196640 | tf_op jit(solution)/shard_map/ppermute | solution.py:367
  85.9 4.6 %collective-permute-done.6.fifth1 = f32[12,32,128]{2,1,0:T(8,128)S(1)} collective-permute-done((f32[12,32,128]{2,1,0:T(8,128)S(1)}, f32[12,32,128]{2,1,0:T(8,128)S(1)}, u32[]{:S(2)}, u32[]{:S(2)}) %collective-permute-start.6) | collective-permute-done | bytes 196640 | tf_op jit(solution)/shard_map/ppermute | solution.py:367
  90.5 3.1 %collective-permute-done.7.fifth2 = f32[12,32,128]{2,1,0:T(8,128)S(1)} collective-permute-done((f32[12,32,128]{2,1,0:T(8,128)S(1)}, f32[12,32,128]{2,1,0:T(8,128)S(1)}, u32[]{:S(2)}, u32[]{:S(2)}) %collective-permute-start.7) | collective-permute-done | bytes 196640 | tf_op jit(solution)/shard_map/ppermute | solution.py:367
  93.6 1.0 %shard_map.48 = f32[24,32,128]{2,1,0:T(8,128)} custom-call(f32[24,32,128]{2,1,0:T(8,128)S(1)} %get-tuple-element.22.v, f32[24,32,128]{2,1,0:T(8,128)S(1)} %get-tuple-element.25.hops_in, f32[1,18,4,8,128]{4,3,2,1,0:T(8,128)S(1)} %get-tuple-element.17.time_links, f32[12,32,128]{2,1,0:T(8,128)S(1)} %collective-permute-done.4.time1, ...), custom_call_target="tpu_custom_call" | custom-call | flops 20000000 | bytes 2260992 | tf_op jit(solution)/shard_map/pallas_call | solution.py:352
Async XLA Ops:
  14.3 15.6 %all-to-all-start.1 = ((f32[8,48,128]{2,1,0:T(8,128)}), f32[8,48,128]{2,1,0:T(8,128)S(1)}, u32[]{:S(2)}, u32[]{:S(2)}) async-start(f32[8,48,128]{2,1,0:T(8,128)} %shard_map.41), calls=%async_computation.1 | async-start | bytes 393216 | tf_op jit(solution)/shard_map/all_to_all | solution.py:371
  22.0 11.4 %copy-start = (f32[2,4,3,1,1,4096]{5,4,3,2,1,0:T(1,128)S(1)}, f32[2,4,3,1,1,4096]{5,4,3,2,1,0:T(1,128)}, u32[]{:S(2)}) copy-start(f32[2,4,3,1,1,4096]{5,4,3,2,1,0:T(1,128)} %param.2) | copy-start | bytes 1179652
  29.9 28.1 %all-to-all-start.2 = ((f32[8,144,128]{2,1,0:T(8,128)}), f32[8,144,128]{2,1,0:T(8,128)S(1)}, u32[]{:S(2)}, u32[]{:S(2)}) async-start(f32[8,144,128]{2,1,0:T(8,128)} %shard_map.42), calls=%async_computation.2 | async-start | bytes 1179648 | tf_op jit(solution)/shard_map/all_to_all | solution.py:371
  33.5 25.4 %collective-permute-start.2 = (f32[12,32,128]{2,1,0:T(8,128)S(1)}, f32[12,32,128]{2,1,0:T(8,128)S(1)}, u32[]{:S(2)}, u32[]{:S(2)}) collective-permute-start(f32[12,32,128]{2,1,0:T(8,128)S(1)} %get-tuple-element.20), channel_id=1, source_target_pairs={{0,1},{1,0},{2,3},{3,2},{4,5},{5,4},{6,7},{7,6},{8,9},{9,8},{10,11... | collective-permute-start | bytes 589832 | tf_op jit(solution)/shard_map/ppermute | solution.py:367
  36.3 22.6 %collective-permute-start.3 = (f32[12,32,128]{2,1,0:T(8,128)S(1)}, f32[12,32,128]{2,1,0:T(8,128)S(1)}, u32[]{:S(2)}, u32[]{:S(2)}) collective-permute-start(f32[12,32,128]{2,1,0:T(8,128)S(1)} %get-tuple-element.21), channel_id=1, source_target_pairs={{0,31},{1,2},{2,1},{3,4},{4,3},{5,6},{6,5},{7,8},{8,7},{9,10},{10,... | collective-permute-start | bytes 589832 | tf_op jit(solution)/shard_map/ppermute | solution.py:367
  41.9 17.0 %collective-permute-start = (f32[12,32,128]{2,1,0:T(8,128)S(1)}, f32[12,32,128]{2,1,0:T(8,128)S(1)}, u32[]{:S(2)}, u32[]{:S(2)}) collective-permute-start(f32[12,32,128]{2,1,0:T(8,128)S(1)} %get-tuple-element.18), channel_id=1, source_target_pairs={{0,32},{32,0},{64,96},{96,64},{128,160},{160,128},{192,224},{224,1... | collective-permute-start | bytes 589832 | tf_op jit(solution)/shard_map/ppermute | solution.py:367
  48.3 18.5 %collective-permute-start.1 = (f32[12,32,128]{2,1,0:T(8,128)S(1)}, f32[12,32,128]{2,1,0:T(8,128)S(1)}, u32[]{:S(2)}, u32[]{:S(2)}) collective-permute-start(f32[12,32,128]{2,1,0:T(8,128)S(1)} %get-tuple-element.19), channel_id=1, source_target_pairs={{0,736},{32,64},{64,32},{96,128},{128,96},{160,192},{192,160},{224... | collective-permute-start | bytes 589832 | tf_op jit(solution)/shard_map/ppermute | solution.py:367
  67.2 17.0 %collective-permute-start.4 = (f32[12,32,128]{2,1,0:T(8,128)S(1)}, f32[12,32,128]{2,1,0:T(8,128)S(1)}, u32[]{:S(2)}, u32[]{:S(2)}) collective-permute-start(f32[12,32,128]{2,1,0:T(8,128)S(1)} %get-tuple-element.26), channel_id=1, source_target_pairs={{0,32},{32,0},{64,96},{96,64},{128,160},{160,128},{192,224},{224,1... | collective-permute-start | bytes 589832 | tf_op jit(solution)/shard_map/ppermute | solution.py:367
  73.9 12.0 %collective-permute-start.5 = (f32[12,32,128]{2,1,0:T(8,128)S(1)}, f32[12,32,128]{2,1,0:T(8,128)S(1)}, u32[]{:S(2)}, u32[]{:S(2)}) collective-permute-start(f32[12,32,128]{2,1,0:T(8,128)S(1)} %get-tuple-element.27), channel_id=1, source_target_pairs={{0,736},{32,64},{64,32},{96,128},{128,96},{160,192},{192,160},{224... | collective-permute-start | bytes 589832 | tf_op jit(solution)/shard_map/ppermute | solution.py:367
  76.4 14.1 %collective-permute-start.6 = (f32[12,32,128]{2,1,0:T(8,128)S(1)}, f32[12,32,128]{2,1,0:T(8,128)S(1)}, u32[]{:S(2)}, u32[]{:S(2)}) collective-permute-start(f32[12,32,128]{2,1,0:T(8,128)S(1)} %get-tuple-element.28), channel_id=1, source_target_pairs={{0,1},{1,0},{2,3},{3,2},{4,5},{5,4},{6,7},{7,6},{8,9},{9,8},{10,11... | collective-permute-start | bytes 589832 | tf_op jit(solution)/shard_map/ppermute | solution.py:367
  78.3 15.3 %collective-permute-start.7 = (f32[12,32,128]{2,1,0:T(8,128)S(1)}, f32[12,32,128]{2,1,0:T(8,128)S(1)}, u32[]{:S(2)}, u32[]{:S(2)}) collective-permute-start(f32[12,32,128]{2,1,0:T(8,128)S(1)} %get-tuple-element.29), channel_id=1, source_target_pairs={{0,31},{1,2},{2,1},{3,4},{4,3},{5,6},{6,5},{7,8},{8,7},{9,10},{10,... | collective-permute-start | bytes 589832 | tf_op jit(solution)/shard_map/ppermute | solution.py:367
where the time goes:
time: 96.2 us; the launch traced here: 94.6 us
  starting transfers between devices  50.2 us (52%)
  waiting for transfers between devices  25.2 us (26%)
  blocking collectives  12.3 us (13%)
  Pallas kernels  5.43 us (6%)
    ppermute x8, starting transfers between devices, trade(): return lax.ppermute(block, axis, route)  39.9 us
    ppermute x8, waiting for transfers between devices, trade(): return lax.ppermute(block, axis, route)  17.3 us
    all_to_all x1, blocking collectives, traded(): lax.all_to_all(copies, 'fifth', 0, 0, axis_index_groups=groups, tiled=False)  12.3 us
    all_to_all x2, starting transfers between devices, traded(): lax.all_to_all(copies, 'fifth', 0, 0, axis_index_groups=groups, tiled=False)  10.4 us
    all_to_all x2, waiting for transfers between devices, traded(): lax.all_to_all(copies, 'fifth', 0, 0, axis_index_groups=groups, tiled=False)  7.87 us
    pallas_call x8, Pallas kernels, run(): pl.pallas_call(kernel, out_shape=outs, in_specs=[vmem] * len(args), out_s...  5.43 us
  transfers between devices with their start and end apart: 10, of which 5 were waited for; matrix products, arithmetic and copies ran while one was open for 0% of the time, Pallas kernels for 4%

commit v1 on v0

--- a/solution.py
+++ b/solution.py
@@ -329,6 +329,17 @@
         put_field(out, k, finish(v, k, hops, (None, time_links), time1, time2, fifth1, fifth2))
 
 
+def run_copies(own, out, held, sem_in, sem_out):
+    load = pltpu.make_async_copy(own, held, sem_in)
+    load.start()
+    load.wait()
+    stores = [pltpu.make_async_copy(held, out.at[i], sem_out.at[i]) for i in range(RUN)]
+    for store in stores:
+        store.start()
+    for store in stores:
+        store.wait()
+
+
 def ring_copies(spans, run_rows, out):
     filled = 0
     for place in range(RUN):
@@ -381,7 +392,15 @@
     count = lax.axis_size("fifth")
     runs = [list(range(i, i + RUN)) for i in range(0, count, RUN)]
     rings = [list(range(i, count, RUN)) for i in range(RUN)]
-    own = jnp.broadcast_to(gauge_rows.reshape(1, 48, 128), (RUN, 48, 128))
+    own = pl.pallas_call(
+        run_copies,
+        out_shape=jax.ShapeDtypeStruct((RUN, 48, 128), F32),
+        in_specs=[pl.BlockSpec(memory_space=pl.ANY)],
+        out_specs=pl.BlockSpec(memory_space=pl.ANY),
+        scratch_shapes=[
+            pltpu.VMEM((48, 128), F32), pltpu.SemaphoreType.DMA, pltpu.SemaphoreType.DMA((RUN,))
+        ],
+    )(gauge_rows.reshape(48, 128))
     run_rows = traded(own, runs)
     time_copies, space_copies = (
         run(

time: 96.2 us -> 97.2 us (1.010)
  Pallas kernels: 5.43 us -> 6.84 us
    pallas_call x0 -> x1, Pallas kernels: none -> 1.41 us  [on_device(): pl.pallas_call(run_copies, out_shape=jax.ShapeDtypeStruct((RUN, 48, 128),...]
  transfers between devices with their start and end apart: 10 -> 10, of which waited for: 5 -> 5; matrix products, arithmetic and copies ran while one was open for 0% -> 0% of each run, Pallas kernels for 4% -> 3%
where the time goes in v1:
time: 97.2 us; the launch traced here: 95.5 us
  starting transfers between devices  50.2 us (52%)
  waiting for transfers between devices  25.2 us (26%)
  blocking collectives  12.5 us (13%)
  Pallas kernels  6.84 us (7%)
    ppermute x8, starting transfers between devices, trade(): return lax.ppermute(block, axis, route)  39.9 us
    ppermute x8, waiting for transfers between devices, trade(): return lax.ppermute(block, axis, route)  17.3 us
    all_to_all x1, blocking collectives, traded(): lax.all_to_all(copies, 'fifth', 0, 0, axis_index_groups=groups, tiled=False)  12.5 us
    all_to_all x2, starting transfers between devices, traded(): lax.all_to_all(copies, 'fifth', 0, 0, axis_index_groups=groups, tiled=False)  10.4 us
    all_to_all x2, waiting for transfers between devices, traded(): lax.all_to_all(copies, 'fifth', 0, 0, axis_index_groups=groups, tiled=False)  7.86 us
    pallas_call x8, Pallas kernels, run(): pl.pallas_call(kernel, out_shape=outs, in_specs=[vmem] * len(args), out_s...  5.43 us
  transfers between devices with their start and end apart: 10, of which 5 were waited for; matrix products, arithmetic and copies ran while one was open for 0% of the time, Pallas kernels for 3%

profile of v1, /device:TPU:1, one launch (start us, length us, event | category | flops | bytes accessed | tf_op | source)
XLA Modules:
  0.0 95.5 jit_solution(15236290164157272428)
XLA Ops:
  0.6 1.4 %shard_map.41 = f32[4,48,128]{2,1,0:T(8,128)} custom-call(f32[48,128]{1,0:T(8,128)} %bitcast.14), custom_call_target="tpu_custom_call" | custom-call | tf_op jit(solution)/shard_map/pallas_call | solution.py:395
  2.0 12.5 %all_to_all.15.run_rows = f32[4,48,128]{2,1,0:T(8,128)S(1)} all-to-all(f32[4,48,128]{2,1,0:T(8,128)} %shard_map.41), channel_id=1, replica_groups={{0,1,2,3},{4,5,6,7},{8,9,10,11},{12,13,14,15},{16,17,18,19},{20,21,22,2..., dimensions={0} | all-to-all | bytes 196608 | tf_op jit(solution)/shard_map/all_to_all | solution.py:382
  14.5 0.7 shard_map.42
  15.2 6.8 %all-to-all-start.1 = ((f32[8,48,128]{2,1,0:T(8,128)}), f32[8,48,128]{2,1,0:T(8,128)S(1)}, u32[]{:S(2)}, u32[]{:S(2)}) async-start(f32[8,48,128]{2,1,0:T(8,128)} %shard_map.42), calls=%async_computation.1 | async-start | bytes 393216 | tf_op jit(solution)/shard_map/all_to_all | solution.py:382
  22.1 0.9 shard_map.43
  22.9 0.0 copy-start
  22.9 7.9 %all-to-all-done.1 = f32[8,48,128]{2,1,0:T(8,128)S(1)} async-done(((f32[8,48,128]{2,1,0:T(8,128)}), f32[8,48,128]{2,1,0:T(8,128)S(1)}, u32[]{:S(2)}, u32[]{:S(2)}) %all-to-all-start.1) | async-done | bytes 196640 | tf_op jit(solution)/shard_map/all_to_all | solution.py:382
  30.8 3.5 %all-to-all-start.2 = ((f32[8,144,128]{2,1,0:T(8,128)}), f32[8,144,128]{2,1,0:T(8,128)S(1)}, u32[]{:S(2)}, u32[]{:S(2)}) async-start(f32[8,144,128]{2,1,0:T(8,128)} %shard_map.43), calls=%async_computation.2 | async-start | bytes 1179648 | tf_op jit(solution)/shard_map/all_to_all | solution.py:382
  34.3 0.0 copy-done
  34.4 2.8 %collective-permute-start.2 = (f32[12,32,128]{2,1,0:T(8,128)S(1)}, f32[12,32,128]{2,1,0:T(8,128)S(1)}, u32[]{:S(2)}, u32[]{:S(2)}) collective-permute-start(f32[12,32,128]{2,1,0:T(8,128)S(1)} %get-tuple-element.20), channel_id=1, source_target_pairs={{0,1},{1,0},{2,3},{3,2},{4,5},{5,4},{6,7},{7,6},{8,9},{9,8},{10,11... | collective-permute-start | bytes 589832 | tf_op jit(solution)/shard_map/ppermute | solution.py:378
  37.2 5.3 %collective-permute-start.3 = (f32[12,32,128]{2,1,0:T(8,128)S(1)}, f32[12,32,128]{2,1,0:T(8,128)S(1)}, u32[]{:S(2)}, u32[]{:S(2)}) collective-permute-start(f32[12,32,128]{2,1,0:T(8,128)S(1)} %get-tuple-element.21), channel_id=1, source_target_pairs={{0,31},{1,2},{2,1},{3,4},{4,3},{5,6},{6,5},{7,8},{8,7},{9,10},{10,... | collective-permute-start | bytes 589832 | tf_op jit(solution)/shard_map/ppermute | solution.py:378
  42.5 0.2 shard_map.45
  42.7 7.1 %collective-permute-start = (f32[12,32,128]{2,1,0:T(8,128)S(1)}, f32[12,32,128]{2,1,0:T(8,128)S(1)}, u32[]{:S(2)}, u32[]{:S(2)}) collective-permute-start(f32[12,32,128]{2,1,0:T(8,128)S(1)} %get-tuple-element.18), channel_id=1, source_target_pairs={{0,32},{32,0},{64,96},{96,64},{128,160},{160,128},{192,224},{224,1... | collective-permute-start | bytes 589832 | tf_op jit(solution)/shard_map/ppermute | solution.py:378
  49.9 9.0 %collective-permute-start.1 = (f32[12,32,128]{2,1,0:T(8,128)S(1)}, f32[12,32,128]{2,1,0:T(8,128)S(1)}, u32[]{:S(2)}, u32[]{:S(2)}) collective-permute-start(f32[12,32,128]{2,1,0:T(8,128)S(1)} %get-tuple-element.19), channel_id=1, source_target_pairs={{0,736},{32,64},{64,32},{96,128},{128,96},{160,192},{192,160},{224... | collective-permute-start | bytes 589832 | tf_op jit(solution)/shard_map/ppermute | solution.py:378
  58.9 0.0 all-to-all-done.2
  58.9 0.9 shard_map.44
  59.8 0.0 collective-permute-done.2.fifth1
  59.8 0.0 collective-permute-done.3.fifth2
  59.8 0.0 collective-permute-done.time1
  59.8 7.9 %collective-permute-done.1.time2 = f32[12,32,128]{2,1,0:T(8,128)S(1)} collective-permute-done((f32[12,32,128]{2,1,0:T(8,128)S(1)}, f32[12,32,128]{2,1,0:T(8,128)S(1)}, u32[]{:S(2)}, u32[]{:S(2)}) %collective-permute-start.1) | collective-permute-done | bytes 196640 | tf_op jit(solution)/shard_map/ppermute | solution.py:378
  67.7 0.4 shard_map.47
  68.1 6.7 %collective-permute-start.4 = (f32[12,32,128]{2,1,0:T(8,128)S(1)}, f32[12,32,128]{2,1,0:T(8,128)S(1)}, u32[]{:S(2)}, u32[]{:S(2)}) collective-permute-start(f32[12,32,128]{2,1,0:T(8,128)S(1)} %get-tuple-element.26), channel_id=1, source_target_pairs={{0,32},{32,0},{64,96},{96,64},{128,160},{160,128},{192,224},{224,1... | collective-permute-start | bytes 589832 | tf_op jit(solution)/shard_map/ppermute | solution.py:378
  74.8 2.5 %collective-permute-start.5 = (f32[12,32,128]{2,1,0:T(8,128)S(1)}, f32[12,32,128]{2,1,0:T(8,128)S(1)}, u32[]{:S(2)}, u32[]{:S(2)}) collective-permute-start(f32[12,32,128]{2,1,0:T(8,128)S(1)} %get-tuple-element.27), channel_id=1, source_target_pairs={{0,736},{32,64},{64,32},{96,128},{128,96},{160,192},{192,160},{224... | collective-permute-start | bytes 589832 | tf_op jit(solution)/shard_map/ppermute | solution.py:378
  77.3 1.9 %collective-permute-start.6 = (f32[12,32,128]{2,1,0:T(8,128)S(1)}, f32[12,32,128]{2,1,0:T(8,128)S(1)}, u32[]{:S(2)}, u32[]{:S(2)}) collective-permute-start(f32[12,32,128]{2,1,0:T(8,128)S(1)} %get-tuple-element.28), channel_id=1, source_target_pairs={{0,1},{1,0},{2,3},{3,2},{4,5},{5,4},{6,7},{7,6},{8,9},{9,8},{10,11... | collective-permute-start | bytes 589832 | tf_op jit(solution)/shard_map/ppermute | solution.py:378
  79.2 4.5 %collective-permute-start.7 = (f32[12,32,128]{2,1,0:T(8,128)S(1)}, f32[12,32,128]{2,1,0:T(8,128)S(1)}, u32[]{:S(2)}, u32[]{:S(2)}) collective-permute-start(f32[12,32,128]{2,1,0:T(8,128)S(1)} %get-tuple-element.29), channel_id=1, source_target_pairs={{0,31},{1,2},{2,1},{3,4},{4,3},{5,6},{6,5},{7,8},{8,7},{9,10},{10,... | collective-permute-start | bytes 589832 | tf_op jit(solution)/shard_map/ppermute | solution.py:378
  83.7 1.4 %shard_map.48 = (f32[24,32,128]{2,1,0:T(8,128)}, f32[24,32,128]{2,1,0:T(8,128)S(1)}) custom-call(f32[24,32,128]{2,1,0:T(8,128)S(1)} %get-tuple-element.22.v, f32[3,18,4,8,128]{4,3,2,1,0:T(8,128)S(1)} %get-tuple-element.23.space_links), custom_call_target="tpu_custom_call" | custom-call | flops 20000000 | bytes 2064384 | tf_op jit(solution)/shard_map/pallas_call | solution.py:363
  85.1 0.0 collective-permute-done.4.time1
  85.1 1.7 %collective-permute-done.5.time2 = f32[12,32,128]{2,1,0:T(8,128)S(1)} collective-permute-done((f32[12,32,128]{2,1,0:T(8,128)S(1)}, f32[12,32,128]{2,1,0:T(8,128)S(1)}, u32[]{:S(2)}, u32[]{:S(2)}) %collective-permute-start.5) | collective-permute-done | bytes 196640 | tf_op jit(solution)/shard_map/ppermute | solution.py:378
  86.8 4.7 %collective-permute-done.6.fifth1 = f32[12,32,128]{2,1,0:T(8,128)S(1)} collective-permute-done((f32[12,32,128]{2,1,0:T(8,128)S(1)}, f32[12,32,128]{2,1,0:T(8,128)S(1)}, u32[]{:S(2)}, u32[]{:S(2)}) %collective-permute-start.6) | collective-permute-done | bytes 196640 | tf_op jit(solution)/shard_map/ppermute | solution.py:378
  91.5 3.0 %collective-permute-done.7.fifth2 = f32[12,32,128]{2,1,0:T(8,128)S(1)} collective-permute-done((f32[12,32,128]{2,1,0:T(8,128)S(1)}, f32[12,32,128]{2,1,0:T(8,128)S(1)}, u32[]{:S(2)}, u32[]{:S(2)}) %collective-permute-start.7) | collective-permute-done | bytes 196640 | tf_op jit(solution)/shard_map/ppermute | solution.py:378
  94.5 1.0 %shard_map.49 = f32[24,32,128]{2,1,0:T(8,128)} custom-call(f32[24,32,128]{2,1,0:T(8,128)S(1)} %get-tuple-element.22.v, f32[24,32,128]{2,1,0:T(8,128)S(1)} %get-tuple-element.25.hops_in, f32[1,18,4,8,128]{4,3,2,1,0:T(8,128)S(1)} %get-tuple-element.17.time_links, f32[12,32,128]{2,1,0:T(8,128)S(1)} %collective-permute-done.4.time1, ...), custom_call_target="tpu_custom_call" | custom-call | flops 20000000 | bytes 2260992 | tf_op jit(solution)/shard_map/pallas_call | solution.py:363
  (1 shorter events, 0.0 us)
Async XLA Ops:
  15.2 15.6 %all-to-all-start.1 = ((f32[8,48,128]{2,1,0:T(8,128)}), f32[8,48,128]{2,1,0:T(8,128)S(1)}, u32[]{:S(2)}, u32[]{:S(2)}) async-start(f32[8,48,128]{2,1,0:T(8,128)} %shard_map.42), calls=%async_computation.1 | async-start | bytes 393216 | tf_op jit(solution)/shard_map/all_to_all | solution.py:382
  22.9 11.4 %copy-start = (f32[2,4,3,1,1,4096]{5,4,3,2,1,0:T(1,128)S(1)}, f32[2,4,3,1,1,4096]{5,4,3,2,1,0:T(1,128)}, u32[]{:S(2)}) copy-start(f32[2,4,3,1,1,4096]{5,4,3,2,1,0:T(1,128)} %param.2) | copy-start | bytes 1179652
  30.8 28.1 %all-to-all-start.2 = ((f32[8,144,128]{2,1,0:T(8,128)}), f32[8,144,128]{2,1,0:T(8,128)S(1)}, u32[]{:S(2)}, u32[]{:S(2)}) async-start(f32[8,144,128]{2,1,0:T(8,128)} %shard_map.43), calls=%async_computation.2 | async-start | bytes 1179648 | tf_op jit(solution)/shard_map/all_to_all | solution.py:382
  34.4 25.4 %collective-permute-start.2 = (f32[12,32,128]{2,1,0:T(8,128)S(1)}, f32[12,32,128]{2,1,0:T(8,128)S(1)}, u32[]{:S(2)}, u32[]{:S(2)}) collective-permute-start(f32[12,32,128]{2,1,0:T(8,128)S(1)} %get-tuple-element.20), channel_id=1, source_target_pairs={{0,1},{1,0},{2,3},{3,2},{4,5},{5,4},{6,7},{7,6},{8,9},{9,8},{10,11... | collective-permute-start | bytes 589832 | tf_op jit(solution)/shard_map/ppermute | solution.py:378
  37.2 22.6 %collective-permute-start.3 = (f32[12,32,128]{2,1,0:T(8,128)S(1)}, f32[12,32,128]{2,1,0:T(8,128)S(1)}, u32[]{:S(2)}, u32[]{:S(2)}) collective-permute-start(f32[12,32,128]{2,1,0:T(8,128)S(1)} %get-tuple-element.21), channel_id=1, source_target_pairs={{0,31},{1,2},{2,1},{3,4},{4,3},{5,6},{6,5},{7,8},{8,7},{9,10},{10,... | collective-permute-start | bytes 589832 | tf_op jit(solution)/shard_map/ppermute | solution.py:378
  42.7 17.1 %collective-permute-start = (f32[12,32,128]{2,1,0:T(8,128)S(1)}, f32[12,32,128]{2,1,0:T(8,128)S(1)}, u32[]{:S(2)}, u32[]{:S(2)}) collective-permute-start(f32[12,32,128]{2,1,0:T(8,128)S(1)} %get-tuple-element.18), channel_id=1, source_target_pairs={{0,32},{32,0},{64,96},{96,64},{128,160},{160,128},{192,224},{224,1... | collective-permute-start | bytes 589832 | tf_op jit(solution)/shard_map/ppermute | solution.py:378
  49.9 17.8 %collective-permute-start.1 = (f32[12,32,128]{2,1,0:T(8,128)S(1)}, f32[12,32,128]{2,1,0:T(8,128)S(1)}, u32[]{:S(2)}, u32[]{:S(2)}) collective-permute-start(f32[12,32,128]{2,1,0:T(8,128)S(1)} %get-tuple-element.19), channel_id=1, source_target_pairs={{0,736},{32,64},{64,32},{96,128},{128,96},{160,192},{192,160},{224... | collective-permute-start | bytes 589832 | tf_op jit(solution)/shard_map/ppermute | solution.py:378
  68.1 17.0 %collective-permute-start.4 = (f32[12,32,128]{2,1,0:T(8,128)S(1)}, f32[12,32,128]{2,1,0:T(8,128)S(1)}, u32[]{:S(2)}, u32[]{:S(2)}) collective-permute-start(f32[12,32,128]{2,1,0:T(8,128)S(1)} %get-tuple-element.26), channel_id=1, source_target_pairs={{0,32},{32,0},{64,96},{96,64},{128,160},{160,128},{192,224},{224,1... | collective-permute-start | bytes 589832 | tf_op jit(solution)/shard_map/ppermute | solution.py:378
  74.8 12.0 %collective-permute-start.5 = (f32[12,32,128]{2,1,0:T(8,128)S(1)}, f32[12,32,128]{2,1,0:T(8,128)S(1)}, u32[]{:S(2)}, u32[]{:S(2)}) collective-permute-start(f32[12,32,128]{2,1,0:T(8,128)S(1)} %get-tuple-element.27), channel_id=1, source_target_pairs={{0,736},{32,64},{64,32},{96,128},{128,96},{160,192},{192,160},{224... | collective-permute-start | bytes 589832 | tf_op jit(solution)/shard_map/ppermute | solution.py:378
  77.3 14.2 %collective-permute-start.6 = (f32[12,32,128]{2,1,0:T(8,128)S(1)}, f32[12,32,128]{2,1,0:T(8,128)S(1)}, u32[]{:S(2)}, u32[]{:S(2)}) collective-permute-start(f32[12,32,128]{2,1,0:T(8,128)S(1)} %get-tuple-element.28), channel_id=1, source_target_pairs={{0,1},{1,0},{2,3},{3,2},{4,5},{5,4},{6,7},{7,6},{8,9},{9,8},{10,11... | collective-permute-start | bytes 589832 | tf_op jit(solution)/shard_map/ppermute | solution.py:378
  79.2 15.3 %collective-permute-start.7 = (f32[12,32,128]{2,1,0:T(8,128)S(1)}, f32[12,32,128]{2,1,0:T(8,128)S(1)}, u32[]{:S(2)}, u32[]{:S(2)}) collective-permute-start(f32[12,32,128]{2,1,0:T(8,128)S(1)} %get-tuple-element.29), channel_id=1, source_target_pairs={{0,31},{1,2},{2,1},{3,4},{4,3},{5,6},{6,5},{7,8},{8,7},{9,10},{10,... | collective-permute-start | bytes 589832 | tf_op jit(solution)/shard_map/ppermute | solution.py:378
